TPU v7x, 512 devices: a whole 4x4x16 slice. The times are simulated.
512 devices in a mesh: dp: 2 (over core), ctx: 32 (over x, z_lo), tensor: 8 (over z_hi, y).
Axes of the slice: x: 4, y: 4, z: 16 (z_hi: 2, z_lo: 8; z = z_hi * 8 + z_lo), core: 2. Of those that a mesh axis runs over, the one named last changes fastest.
Arguments:
- tokens: bfloat16 [2, 4096, 2048], P('dp', 'ctx', 'tensor'), may hold values from -6 to 6
- cotangent: bfloat16 [2, 4096, 2048], P('dp', 'ctx', 'tensor'), may hold values from -6 to 6
- w_value: bfloat16 [2048, 2048], P('ctx', 'tensor'), may hold values from -0.125 to 0.125
- w_gate: bfloat16 [2048, 2048], P('ctx', 'tensor'), may hold values from -0.125 to 0.125
- decay_rate: float32 [4, 2048], P(None, 'tensor'), as said below
- residue: float32 [4, 2048], P(None, 'tensor'), may hold values from -4 to 4
- skip_gain: float32 [2048], P('tensor'), may hold values from -4 to 4
- contig_len: int32 [2, 8], P('dp'), may hold values from 1 to 1536, 4096 in all within a row
Outputs:
- output: bfloat16 [2, 4096, 2048], P('dp', 'ctx', 'tensor')
- grad_tokens: bfloat16 [2, 4096, 2048], P('dp', 'ctx', 'tensor')
- grad_w_value: float32 [2048, 2048], P('ctx', 'tensor')
- grad_w_gate: float32 [2048, 2048], P('ctx', 'tensor')
- grad_skip: float32 [2048], P('tensor')
- grad_residue: float32 [4, 2048], P(None, 'tensor')
- grad_rate: float32 [4, 2048], P(None, 'tensor')
Inputs may be any that keep to these rules, and one draw needn't show every extreme that they name: `contig_len`: each row's lengths sum to 4096; the largest of each row is exactly 1536. `decay_rate`: every rate lies between 0.25 / 4096 and 1 / 30.
All inputs are finite; a program needn't handle non-finite values.
Results may differ from a plain program's by a relative error of at most 0.012.
Values may be sent and summed in bfloat16 or wider, within the bound.
A program may use at most 64 MiB of HBM per device.

v0:
```python
import jax
import jax.numpy as jnp
from jax import lax
from jax.sharding import PartitionSpec as P


def carried_in(part, axis, combine, identity, reverse):
    count = lax.axis_size(axis)
    place = lax.axis_index(axis)
    ahead = count - 1 - place if reverse else place
    gathered = jax.tree.map(lambda a: lax.all_gather(a, axis), part)
    state = jax.tree.map(lambda a, e: jnp.zeros_like(a) + jnp.asarray(e, a.dtype), part, identity)

    def one(hop, state):
        source = count - 1 - hop if reverse else hop
        return combine(
            state, jax.tree.map(lambda a: lax.dynamic_index_in_dim(a, source, 0, False), gathered)
        )

    return lax.fori_loop(0, ahead, one, state)


def link(first, second):
    return (first[0] * second[0], second[0] * first[1] + second[1])


def body(tokens, cotangent, w_value, w_gate, decay_rate, residue, skip_gain, contig_len):
    rows, span, width = tokens.shape
    flat = tokens.reshape(rows * span, width)
    feats = lax.all_gather(flat, "tensor", axis=1, tiled=True)
    paired_w = jnp.concatenate([w_value, w_gate], axis=1)
    whole = lax.all_gather(paired_w, "ctx", axis=0, tiled=True)
    both = jnp.dot(feats, whole, preferred_element_type=jnp.float32)
    value = both[:, :width].reshape(rows, span, width)
    gate = both[:, width:].reshape(rows, span, width)
    me = lax.axis_index("ctx")
    first = me * span
    positions = first + jnp.arange(span, dtype=jnp.int32)
    starts = jnp.cumsum(contig_len, axis=1) - contig_len
    here = starts[:, None, :]
    place = positions[None, :, None]
    reset = jnp.any(place == here, axis=2).astype(jnp.float32)
    reset_next = jnp.any(place + 1 == here, axis=2).astype(jnp.float32)
    clear_fwd = jnp.all((here < first) | (here > place), axis=2).astype(jnp.float32)
    clear_back = jnp.all((here <= place) | (here > first + span), axis=2).astype(jnp.float32)
    pole = jnp.exp(-decay_rate)
    factor = jnp.sqrt(-jnp.expm1(-2.0 * decay_rate))
    weight_mode = residue * factor
    steps_in = (jnp.arange(span, dtype=jnp.int32) + 1).astype(jnp.float32)
    decay_fwd = jnp.exp(-decay_rate[None] * steps_in[:, None, None])
    decay_back = decay_fwd[::-1]
    keep = (1.0 - reset)[:, :, None, None] * pole
    drive = jnp.broadcast_to(value[:, :, None, :], keep.shape)
    local = lax.associative_scan(link, (keep, drive), axis=1)[1]
    scale_end = decay_fwd[-1][None] * clear_fwd[:, -1][:, None, None]
    end_state = local[:, -1]
    _, incoming = carried_in(
        (scale_end, end_state),
        "ctx",
        link,
        (jnp.ones_like(scale_end), jnp.zeros_like(end_state)),
        False,
    )
    state = local + decay_fwd[None] * clear_fwd[:, :, None, None] * incoming[:, None]
    mixed = jnp.sum(weight_mode * state, axis=2) + skip_gain * value
    output = (gate * mixed).astype(jnp.bfloat16)
    upstream = cotangent.astype(jnp.float32)
    grad_mixed = upstream * gate
    grad_gate = upstream * mixed
    keep_back = (1.0 - reset_next)[:, :, None, None] * pole
    source = grad_mixed[:, :, None, :] * weight_mode
    local_back = lax.associative_scan(link, (keep_back[:, ::-1], source[:, ::-1]), axis=1)[1][
        :, ::-1
    ]
    scale_top = decay_back[0][None] * clear_back[:, 0][:, None, None]
    top_state = local_back[:, 0]
    _, incoming_back = carried_in(
        (scale_top, top_state),
        "ctx",
        link,
        (jnp.ones_like(scale_top), jnp.zeros_like(top_state)),
        True,
    )
    grad_state = (
        local_back + decay_back[None] * clear_back[:, :, None, None] * incoming_back[:, None]
    )
    grad_value = jnp.sum(grad_state, axis=2) + skip_gain * grad_mixed
    skip_part = jnp.sum(grad_mixed * value, axis=(0, 1))
    paired_part = jnp.sum(grad_mixed[:, :, None, :] * state, axis=(0, 1))
    carried_part = jnp.sum(grad_state * (state - drive), axis=(0, 1))
    grad_skip, paired, carried = lax.psum((skip_part, paired_part, carried_part), ("dp", "ctx"))
    grad_residue = factor * paired
    grad_rate = -carried + residue * jnp.exp(-2.0 * decay_rate) / factor * paired
    cot_both = (
        jnp.concatenate([grad_value, grad_gate], axis=2)
        .astype(jnp.bfloat16)
        .reshape(rows * span, 2 * width)
    )
    contract = (((1,), (1,)), ((), ()))
    term = lax.dot_general(cot_both, whole, contract, preferred_element_type=jnp.float32)
    grad_tokens = lax.psum_scatter(
        term.astype(jnp.bfloat16), "tensor", scatter_dimension=1, tiled=True
    )
    grad_tokens = grad_tokens.reshape(rows, span, width)
    slabs = lax.all_to_all(feats, "ctx", split_axis=1, concat_axis=0, tiled=True)
    grad_w = lax.dot_general(
        slabs,
        lax.all_gather(cot_both, "ctx", axis=0, tiled=True),
        (((0,), (0,)), ((), ())),
        preferred_element_type=jnp.float32,
    )
    grad_w = lax.psum(grad_w, "dp")
    return (
        output,
        grad_tokens,
        grad_w[:, :width],
        grad_w[:, width:],
        grad_skip,
        grad_residue,
        grad_rate,
    )


def solution(mesh):
    in_specs = (
        P("dp", "ctx", "tensor"),
        P("dp", "ctx", "tensor"),
        P("ctx", "tensor"),
        P("ctx", "tensor"),
        P(None, "tensor"),
        P(None, "tensor"),
        P("tensor"),
        P("dp", None),
    )
    out_specs = (
        P("dp", "ctx", "tensor"),
        P("dp", "ctx", "tensor"),
        P("ctx", "tensor"),
        P("ctx", "tensor"),
        P("tensor"),
        P(None, "tensor"),
        P(None, "tensor"),
    )
    return jax.shard_map(body, mesh=mesh, in_specs=in_specs, out_specs=out_specs, check_vma=False)
```

profile of v0, /device:TPU:17, one launch (start us, length us, event | category | flops | bytes accessed | tf_op | source)
XLA Modules:
  0.0 1120.3 jit_solution(10773666285794444207)
XLA Ops:
  7.2 1.4 pad_maximum_fusion.5
  8.7 0.8 reduce_window_sum.11
  12.6 1.0 copy.23
  16.0 117.6 %all-gather.2 = f32[32,4,256]{2,1,0:T(4,128)} all-gather(f32[1,4,256]{2,1,0:T(4,128)S(1)} %get-tuple-element.204), channel_id=4, replica_groups=mesh['dp'=2,'ctx'=32,'tensor'=8] {'ctx'}, dimensions={0}, use_global_device_ids=true | all-gather | bytes 135168 | tf_op jit(solution)/shard_map/all_gather | solution.py:11
  133.6 104.2 %all-gather.1 = f32[32,4,256]{2,1,0:T(4,128)} all-gather(f32[1,4,256]{2,1,0:T(4,128)S(1)} %get-tuple-element.205), channel_id=3, replica_groups=mesh['dp'=2,'ctx'=32,'tensor'=8] {'ctx'}, dimensions={0}, use_global_device_ids=true | all-gather | bytes 135168 | tf_op jit(solution)/shard_map/all_gather | solution.py:11
  237.8 53.8 %all-gather = bf16[1,128,2048]{1,2,0:T(8,128)(2,1)S(1)} all-gather(bf16[1,128,256]{1,2,0:T(8,128)(2,1)S(1)} %copy.23), channel_id=2, replica_groups=mesh['dp'=2,'ctx'=32,'tensor'=8] {'tensor'}, dimensions={2}, use_global_device_ids=true | all-gather | bytes 589824 | tf_op jit(solution)/shard_map/all_gather | solution.py:30
  291.7 2.1 convolution_bitcast_fusion
  301.4 0.8 pad.112
  302.2 0.8 pad.113
  303.8 1.0 slice_multiply_fusion
  310.6 101.0 %all_gather.34 = f32[32,1,4,256]{3,2,1,0:T(4,128)S(1)} all-gather(f32[1,1,4,256]{3,2,1,0:T(4,128)} %slice_add_fusion.10), channel_id=1, replica_groups=mesh['dp'=2,'ctx'=32,'tensor'=8] {'ctx'}, dimensions={0}, use_global_device_ids=true | all-gather | bytes 135168 | tf_op jit(solution)/shard_map/all_gather | solution.py:11
  411.6 21.3 %while.27 = (s32[]{:T(128)}, f32[1,4,256]{2,1,0:T(4,128)S(1)}, s32[]{:T(128)}, f32[32,1,4,256]{3,2,1,0:T(4,128)}, f32[32,1,4,256]{3,2,1,0:T(4,128)S(1)}, /*index=5*/s32[]{:T(128)}, s32[]{:T(128)}, s32[]{:T(128)}, s32[]{:T(128)}) while((s32[]{:T(128)}, f32[1,4,256]{2,1,0:T(4,128)S(1)}, s32[]{:T(128)}, f32[32,1,4,256]{3,2,1,0:T(4,128)}, ...), condition=%wide.region_9.10_spmd, body=%wide.region_8.9_spmd.sunk | while | flops 2054 | bytes 16535 | solution.py:20
  433.0 0.9 pad_maximum_fusion.2
  435.5 1.0 fusion.4
  437.2 0.8 pad.98
  438.1 22.1 %pad.99 = f32[1,128,4,256]{3,2,1,0:T(4,128)S(1)} pad(f32[1,64,4,256]{3,2,1,0:T(4,128)} %add.297, f32[]{:T(128)} %constant.69.clone.1), padding=0_0_0x1_0_1x0_0_0x0_0_0 | pad | bytes 786436 | tf_op jit(solution)/shard_map/pad | solution.py:54
  460.2 98.4 %all_gather.31 = f32[32,1,4,256]{3,2,1,0:T(4,128)S(1)} all-gather(f32[1,1,4,256]{3,2,1,0:T(4,128)S(1)} %slice_add_fusion.12), channel_id=1, replica_groups=mesh['dp'=2,'ctx'=32,'tensor'=8] {'ctx'}, dimensions={0}, use_global_device_ids=true | all-gather | bytes 135168 | tf_op jit(solution)/shard_map/all_gather | solution.py:11
  558.6 2.3 multiply_reduce_fusion
  561.8 44.6 %all_to_all.19 = bf16[128,32,64]{0,2,1:T(8,128)(2,1)S(1)} all-to-all(bf16[128,32,64]{0,2,1:T(8,128)(2,1)S(1)} %bitcast.93), channel_id=1, replica_groups=mesh['dp'=2,'ctx'=32,'tensor'=8] {'ctx'}, dimensions={1} | all-to-all | bytes 1048576 | tf_op jit(solution)/shard_map/all_to_all | solution.py:105
  606.4 246.9 %all-gather.8.cloned.1.call-done = bf16[4096,512]{1,0:T(8,128)(2,1)} async-done(((bf16[128,512]{1,0:T(8,128)(2,1)}), bf16[4096,512]{1,0:T(8,128)(2,1)}) %all-gather.8.cloned.1.call-update) | async-done | bytes 4194320 | tf_op jit(solution)/shard_map/all_gather | solution.py:108
  853.3 3.7 convolution_bitcast_fusion.1
  857.1 1.6 convolution_convert_fusion
  858.7 252.3 %all-reduce.28 = (f32[256]{0:T(256)}, f32[4,256]{1,0:T(4,128)S(1)}, f32[4,256]{1,0:T(4,128)S(1)}) all-reduce(f32[256]{0:T(256)S(1)} %get-tuple-element.210, f32[4,256]{1,0:T(4,128)S(1)} %get-tuple-element.169, f32[4,256]{1,0:T(4,128)S(1)} %get-tuple-element.167), channel_id=1, replica_groups=mesh['dp'=2,'ctx'=32,'tensor'=8] {'dp','ctx'}, use_global_device_ids=true, to_apply=%region_14.15 | all-reduce | flops 2304 | bytes 18432 | tf_op jit(solution)/shard_map/psum | solution.py:91
  1112.3 1.5 fusion.33
  (179 shorter events, 44.5 us)
Async XLA Ops:
  7.2 284.6 %all-gather.6.cloned.1.call-start = ((), (), s32[]{:S(2)}) async-start(), calls=%async_computation.2 | async-start | bytes 2162688 | tf_op jit(solution)/shard_map/all_gather | solution.py:32
  8.6 844.6 %all-gather.8.cloned.1.call-start = ((), (), s32[]{:S(2)}) async-start(), calls=%async_computation.4 | async-start | bytes 4325376 | tf_op jit(solution)/shard_map/all_gather | solution.py:108
  15.4 0.6 copy-start.10
  291.7 4.7 copy-start.5
  296.4 0.9 copy-start.2
  296.5 1.7 copy-start
  298.6 2.5 copy-start.3
  298.6 2.5 copy-start.4
  300.0 1.3 slice-start
  434.7 123.9 %copy-start.11 = (f32[128]{0:T(128)S(1)}, f32[128]{0:T(128)}, u32[]{:S(2)}) copy-start(f32[128]{0:T(128)} %copy-done.10) | copy-start | bytes 1540
  438.1 122.9 %copy-start.6 = (bf16[1,128,256]{2,1,0:T(8,128)(2,1)S(1)}, bf16[1,128,256]{2,1,0:T(8,128)(2,1)}, u32[]{:S(2)}) copy-start(bf16[1,128,256]{2,1,0:T(8,128)(2,1)} %param.13) | copy-start | bytes 196612
  438.1 122.9 %copy-start.9 = (f32[256]{0:T(256)S(1)}, f32[256]{0:T(256)}, u32[]{:S(2)}) copy-start(f32[256]{0:T(256)} %param.18) | copy-start | bytes 3076
  561.7 550.6 %all-reduce.31.cloned.1.call-start = ((), (), s32[]{:S(2)}) async-start(), calls=%async_computation.5 | async-start | bytes 262144 | tf_op jit(solution)/shard_map/psum | solution.py:112
  606.4 250.7 %copy-start.1 = (bf16[2048,512]{1,0:T(8,128)(2,1)S(1)}, bf16[2048,512]{1,0:T(8,128)(2,1)}, u32[]{:S(2)}) copy-start(bf16[2048,512]{1,0:T(8,128)(2,1)} %all-gather.6.cloned.1.call-done) | copy-start | bytes 6291460
  857.0 254.0 %copy-start.7 = (f32[4,256]{1,0:T(4,128)S(1)}, f32[4,256]{1,0:T(4,128)}, u32[]{:S(2)}) copy-start(f32[4,256]{1,0:T(4,128)} %param.17) | copy-start | bytes 12292
  857.0 254.0 %copy-start.8 = (f32[4,256]{1,0:T(4,128)S(1)}, f32[4,256]{1,0:T(4,128)}, u32[]{:S(2)}) copy-start(f32[4,256]{1,0:T(4,128)} %param.16) | copy-start | bytes 12292
  857.0 256.8 %reduce-scatter.2.cloned.1.call-start = ((), (), s32[]{:S(2)}) async-start(), calls=%async_computation.3 | async-start | bytes 589824 | tf_op jit(solution)/shard_map/reduce_scatter | solution.py:101
Sparse Core Ops, SparseCore 0:
  10.6 209.9 all-gather.5
  561.8 291.4 all-gather.7
  857.1 59.6 all-reduce.30
  921.7 110.2 reduce-scatter.1
where the time goes:
time: 1120 us
  blocking collectives  772 us (69%)
  waiting for transfers between devices  247 us (22%)
  other arithmetic  40.2 us (4%)
  local copies, waits for them, and re-layouts  38.6 us (3%)
  between operations  15 us (1%)
    all_gather x4, blocking collectives, carried_in(): gathered = jax.tree.map(lambda a: lax.all_gather(a, axis), part)  421 us
    psum x1, blocking collectives, body(): lax.psum((skip_part, paired_part, carried_part), ('dp', 'ctx'))  252 us
    all_gather x1, waiting for transfers between devices, body(): lax.all_gather(cot_both, 'ctx', axis=0, tiled=True)  247 us
    all_gather x1, blocking collectives, body(): feats = lax.all_gather(flat, 'tensor', axis=1, tiled=True)  53.8 us
    all_to_all x1, blocking collectives, body(): lax.all_to_all(feats, 'ctx', split_axis=1, concat_axis=0, tiled=True)  44.6 us
    pad x12, local copies, waits for them, and re-layouts, body(): local = lax.associative_scan(link, (keep, drive), axis=1)[1]  24.6 us
    add x42, other arithmetic, link(): return (first[0] * second[0], second[0] * first[1] + second[1])  23.3 us
  transfers between devices with their start and end apart: 4, of which 1 were waited for; matrix products, arithmetic and copies ran while one was open for 1% of the time, Pallas kernels for 0%

commit v1 on v0

--- a/solution.py
+++ b/solution.py
@@ -105,7 +105,9 @@
     slabs = lax.all_to_all(feats, "ctx", split_axis=1, concat_axis=0, tiled=True)
     grad_w = lax.dot_general(
         slabs,
-        lax.all_gather(cot_both, "ctx", axis=0, tiled=True),
+        jnp.concatenate(
+            lax.all_to_all(jnp.stack([cot_both] * lax.axis_size("ctx")), "ctx", 0, 0), axis=0
+        ),
         (((0,), (0,)), ((), ())),
         preferred_element_type=jnp.float32,
     )

time: 1120 us -> 986 us (0.88)
  the two profiles are of different devices: /device:TPU:17 before, /device:TPU:25 now
where the time goes in v1:
time: 986 us; the launch traced here: 984 us
  blocking collectives  899 us (91%)
  other arithmetic  33.4 us (3%)
  local copies, waits for them, and re-layouts  17.4 us (2%)
  between operations  15.1 us (2%)
  starting transfers between devices  14 us (1%)
    all_gather x4, blocking collectives, carried_in(): gathered = jax.tree.map(lambda a: lax.all_gather(a, axis), part)  422 us
    psum x1, blocking collectives, body(): lax.psum((skip_part, paired_part, carried_part), ('dp', 'ctx'))  242 us
    all_to_all x1, blocking collectives, body(): lax.all_to_all(jnp.stack([cot_both] * lax.axis_size('ctx')), 'ctx', 0, 0)  170 us
    all_gather x1, blocking collectives, body(): feats = lax.all_gather(flat, 'tensor', axis=1, tiled=True)  64.5 us
    add x42, other arithmetic, link(): return (first[0] * second[0], second[0] * first[1] + second[1])  22.9 us
  transfers between devices with their start and end apart: 4, of which 0 were waited for; matrix products, arithmetic and copies ran while one was open for 5% of the time, Pallas kernels for 0%

profile of v1, /device:TPU:25, one launch (start us, length us, event | category | flops | bytes accessed | tf_op | source)
XLA Modules:
  0.0 983.8 jit_solution(14726727241982091840)
XLA Ops:
  7.2 1.4 pad_maximum_fusion.5
  8.7 64.5 %all-gather = bf16[1,128,2048]{2,1,0:T(8,128)(2,1)S(1)} all-gather(bf16[1,128,256]{2,1,0:T(8,128)(2,1)} %param.12), channel_id=2, replica_groups=mesh['dp'=2,'ctx'=32,'tensor'=8] {'tensor'}, dimensions={2}, use_global_device_ids=true | all-gather | bytes 589824 | tf_op jit(solution)/shard_map/all_gather | solution.py:30
  73.2 1.0 copy.22
  74.2 13.8 %all-to-all-start.1 = ((bf16[128,32,64]{0,2,1:T(8,128)(2,1)}), bf16[128,32,64]{0,2,1:T(8,128)(2,1)S(1)}, u32[]{:S(2)}, u32[]{:S(2)}) async-start(bf16[128,32,64]{0,2,1:T(8,128)(2,1)} %bitcast.27), calls=%async_computation.2 | async-start | bytes 1048576 | tf_op jit(solution)/shard_map/all_to_all | solution.py:105
  92.4 114.6 %all-gather.2 = f32[32,4,256]{2,1,0:T(4,128)} all-gather(f32[1,4,256]{2,1,0:T(4,128)S(1)} %get-tuple-element.199), channel_id=4, replica_groups=mesh['dp'=2,'ctx'=32,'tensor'=8] {'ctx'}, dimensions={0}, use_global_device_ids=true | all-gather | bytes 135168 | tf_op jit(solution)/shard_map/all_gather | solution.py:11
  207.0 103.3 %all-gather.1 = f32[32,4,256]{2,1,0:T(4,128)} all-gather(f32[1,4,256]{2,1,0:T(4,128)S(1)} %get-tuple-element.200), channel_id=3, replica_groups=mesh['dp'=2,'ctx'=32,'tensor'=8] {'ctx'}, dimensions={0}, use_global_device_ids=true | all-gather | bytes 135168 | tf_op jit(solution)/shard_map/all_gather | solution.py:11
  310.4 2.0 convolution_bitcast_fusion
  315.1 0.8 slice.489
  318.7 0.8 pad.112
  319.5 0.8 pad.113
  320.5 1.0 slice_multiply_fusion
  326.7 104.7 %all_gather.31 = f32[32,1,4,256]{3,2,1,0:T(4,128)} all-gather(f32[1,1,4,256]{3,2,1,0:T(4,128)S(1)} %slice_add_fusion.10), channel_id=1, replica_groups=mesh['dp'=2,'ctx'=32,'tensor'=8] {'ctx'}, dimensions={0}, use_global_device_ids=true | all-gather | bytes 135168 | tf_op jit(solution)/shard_map/all_gather | solution.py:11
  432.4 1.0 fusion.3
  434.2 0.8 pad.98
  435.0 0.8 pad.99
  435.9 99.0 %all_gather.28 = f32[32,1,4,256]{3,2,1,0:T(4,128)S(1)} all-gather(f32[1,1,4,256]{3,2,1,0:T(4,128)S(1)} %slice_add_fusion.12), channel_id=1, replica_groups=mesh['dp'=2,'ctx'=32,'tensor'=8] {'ctx'}, dimensions={0}, use_global_device_ids=true | all-gather | bytes 135168 | tf_op jit(solution)/shard_map/all_gather | solution.py:11
  534.9 21.5 %while.27 = (s32[]{:T(128)}, f32[1,4,256]{2,1,0:T(4,128)S(1)}, s32[]{:T(128)}, f32[32,1,4,256]{3,2,1,0:T(4,128)}, f32[32,1,4,256]{3,2,1,0:T(4,128)}, /*index=5*/s32[]{:T(128)}, s32[]{:T(128)}, s32[]{:T(128)}, s32[]{:T(128)}) while((s32[]{:T(128)}, f32[1,4,256]{2,1,0:T(4,128)S(1)}, s32[]{:T(128)}, f32[32,1,4,256]{3,2,1,0:T(4,128)}, ...), condition=%wide.region_9.10_spmd, body=%wide.region_8.9_spmd.sunk | while | flops 2054 | bytes 16535 | solution.py:20
  554.3 0.7 bitcast_add_fusion.7
  556.4 1.4 multiply_reduce_fusion
  558.5 170.3 %all_to_all.21 = bf16[32,128,512]{2,1,0:T(8,128)(2,1)S(1)} all-to-all(bf16[32,128,512]{2,1,0:T(8,128)(2,1)S(1)} %stack.3), channel_id=1, replica_groups=mesh['dp'=2,'ctx'=32,'tensor'=8] {'ctx'}, dimensions={0} | all-to-all | bytes 8388608 | tf_op jit(solution)/shard_map/all_to_all | solution.py:109
  728.8 1.5 convolution_bitcast_fusion.1
  730.4 1.6 convolution_convert_fusion
  732.0 242.4 %all-reduce.28 = (f32[256]{0:T(256)}, f32[4,256]{1,0:T(4,128)S(1)}, f32[4,256]{1,0:T(4,128)S(1)}) all-reduce(f32[256]{0:T(256)S(1)} %get-tuple-element.205, f32[4,256]{1,0:T(4,128)S(1)} %get-tuple-element.164, f32[4,256]{1,0:T(4,128)S(1)} %get-tuple-element.162), channel_id=1, replica_groups=mesh['dp'=2,'ctx'=32,'tensor'=8] {'dp','ctx'}, use_global_device_ids=true, to_apply=%region_14.15 | all-reduce | flops 2304 | bytes 18432 | tf_op jit(solution)/shard_map/psum | solution.py:91
  975.7 1.5 fusion.32
  (197 shorter events, 38.7 us)
Async XLA Ops:
  7.2 80.9 %copy-start.18 = (s32[1,8]{1,0:T(1,128)S(1)}, s32[1,8]{1,0:T(1,128)}, u32[]{:S(2)}) copy-start(s32[1,8]{1,0:T(1,128)} %param.19) | copy-start | bytes 100
  7.2 83.6 %copy-start.10 = (f32[4,256]{1,0:T(4,128)S(1)}, f32[4,256]{1,0:T(4,128)}, u32[]{:S(2)}) copy-start(f32[4,256]{1,0:T(4,128)} %param.17) | copy-start | bytes 12292
  7.2 83.6 %copy-start.12 = (f32[4,256]{1,0:T(4,128)S(1)}, f32[4,256]{1,0:T(4,128)}, u32[]{:S(2)}) copy-start(f32[4,256]{1,0:T(4,128)} %param.16) | copy-start | bytes 12292
  7.2 303.2 %all-gather.5.cloned.1.call-start = ((), (), s32[]{:S(2)}) async-start(), calls=%async_computation.3 | async-start | bytes 2162688 | tf_op jit(solution)/shard_map/all_gather | solution.py:32
  74.2 483.8 %all-to-all-start.1 = ((bf16[128,32,64]{0,2,1:T(8,128)(2,1)}), bf16[128,32,64]{0,2,1:T(8,128)(2,1)S(1)}, u32[]{:S(2)}, u32[]{:S(2)}) async-start(bf16[128,32,64]{0,2,1:T(8,128)(2,1)} %bitcast.27), calls=%async_computation.2 | async-start | bytes 1048576 | tf_op jit(solution)/shard_map/all_to_all | solution.py:105
  88.0 887.7 %all-reduce.31.cloned.1.call-start = ((), (), s32[]{:S(2)}) async-start(), calls=%async_computation.5 | async-start | bytes 262144 | tf_op jit(solution)/shard_map/psum | solution.py:114
  310.3 4.6 copy-start.8
  315.0 0.9 copy-start.2
  315.1 1.1 copy-start.1
  316.6 1.9 copy-start.6
  316.6 1.9 copy-start.7
  317.4 1.3 slice-start
  432.4 124.0 %copy-start.3 = (f32[128,256]{1,0:T(8,128)S(1)}, f32[128,256]{1,0:T(8,128)}, u32[]{:S(2)}) copy-start(f32[128,256]{1,0:T(8,128)} %copy-done.2) | copy-start | bytes 393220
  432.4 124.0 %copy-start.17 = (f32[128]{0:T(128)S(1)}, f32[128]{0:T(128)}, u32[]{:S(2)}) copy-start(f32[128]{0:T(128)} %copy-done.16) | copy-start | bytes 1540
  432.4 124.0 %copy-start.19 = (f32[128]{0:T(128)S(1)}, f32[128]{0:T(128)}, u32[]{:S(2)}) copy-start(f32[128]{0:T(128)} %convert_element_type.88) | copy-start | bytes 1540
  432.4 124.0 %copy-start.20 = (f32[128]{0:T(128)S(1)}, f32[128]{0:T(128)}, u32[]{:S(2)}) copy-start(f32[128]{0:T(128)} %convert_element_type.82) | copy-start | bytes 1540
  435.0 122.8 %copy-start.9 = (bf16[1,128,256]{2,1,0:T(8,128)(2,1)S(1)}, bf16[1,128,256]{2,1,0:T(8,128)(2,1)}, u32[]{:S(2)}) copy-start(bf16[1,128,256]{2,1,0:T(8,128)(2,1)} %param.13) | copy-start | bytes 196612
  435.0 122.8 %copy-start.14 = (f32[256]{0:T(256)S(1)}, f32[256]{0:T(256)}, u32[]{:S(2)}) copy-start(f32[256]{0:T(256)} %param.18) | copy-start | bytes 3076
  728.8 1.6 copy-start
  730.3 244.1 %copy-start.11 = (f32[4,256]{1,0:T(4,128)S(1)}, f32[4,256]{1,0:T(4,128)}, u32[]{:S(2)}) copy-start(f32[4,256]{1,0:T(4,128)} %param.17) | copy-start | bytes 12292
  730.3 244.1 %copy-start.13 = (f32[4,256]{1,0:T(4,128)S(1)}, f32[4,256]{1,0:T(4,128)}, u32[]{:S(2)}) copy-start(f32[4,256]{1,0:T(4,128)} %param.16) | copy-start | bytes 12292
  730.3 244.8 %copy-start.5 = (f32[128,256]{1,0:T(8,128)S(1)}, f32[128,256]{1,0:T(8,128)}, u32[]{:S(2)}) copy-start(f32[128,256]{1,0:T(8,128)} %copy-done.4) | copy-start | bytes 393220
  730.3 244.8 %copy-start.15 = (f32[256]{0:T(256)S(1)}, f32[256]{0:T(256)}, u32[]{:S(2)}) copy-start(f32[256]{0:T(256)} %param.18) | copy-start | bytes 3076
  730.3 246.9 %reduce-scatter.2.cloned.1.call-start = ((), (), s32[]{:S(2)}) async-start(), calls=%async_computation.4 | async-start | bytes 589824 | tf_op jit(solution)/shard_map/reduce_scatter | solution.py:101
  (2 other events, 1.2 us)
Sparse Core Ops, SparseCore 0:
  10.7 215.2 all-gather.4
  730.4 53.1 all-reduce.30
  788.7 112.0 reduce-scatter.1
